TPU v7x, 32 devices: a whole 2x2x4 slice. The times are simulated.
32 devices in a mesh: dp: 8 (over z, x), shard: 4 (over y, core).
Axes of the slice: x: 2, y: 2, z: 4, core: 2. Of those that a mesh axis runs over, the one named last changes fastest.
Arguments:
- tokens: bfloat16 [8192, 2048], P('dp'), may hold values from -6 to 6
- block_ids: int32 [8, 1024], P('dp'), may hold values from 0 to 7, never falling along the last dimension, each value on 1 to 256 neighbouring positions
- cotangent: bfloat16 [8192, 2048], P('dp'), may hold values from -12 to 12
- gain_first: float32 [2048], P('dp'), may hold values from 0.3 to 2.5
- w_query: float32 [2048, 2048], P('dp', 'shard'), may hold values from -0.125 to 0.125
- w_key: float32 [2048, 512], P('dp', 'shard'), may hold values from -0.125 to 0.125
- w_value: float32 [2048, 512], P('dp', 'shard'), may hold values from -0.125 to 0.125
- w_output: float32 [2048, 2048], P('shard', 'dp'), may hold values from -2 to 2
- gain_second: float32 [2048], P('dp'), may hold values from 0.3 to 2.5
- w_gate: float32 [2048, 8192], P('dp', 'shard'), may hold values from -0.125 to 0.125
- w_up: float32 [2048, 8192], P('dp', 'shard'), may hold values from -0.125 to 0.125
- w_down: float32 [8192, 2048], P('shard', 'dp'), may hold values from -0.0625 to 0.0625
- moment_first: float32 [2048], P('dp'), may hold values from -6 to 6
- moment_query: float32 [2048, 2048], P('dp', 'shard'), may hold values from -4 to 4
- moment_key: float32 [2048, 512], P('dp', 'shard'), may hold values from -4 to 4
- moment_value: float32 [2048, 512], P('dp', 'shard'), may hold values from -4 to 4
- moment_output: float32 [2048, 2048], P('shard', 'dp'), may hold values from -4 to 4
- moment_second: float32 [2048], P('dp'), may hold values from -6 to 6
- moment_gate: float32 [2048, 8192], P('dp', 'shard'), may hold values from -4 to 4
- moment_up: float32 [2048, 8192], P('dp', 'shard'), may hold values from -4 to 4
- moment_down: float32 [8192, 2048], P('shard', 'dp'), may hold values from -4 to 4
- step: int32 [], replicated, may hold values from 1000 to 1999
- rate: float32 [], replicated, may hold values from 0.6 to 1.2
Outputs:
- output: bfloat16 [8192, 2048], P('dp')
- input_grad: float32 [8192, 2048], P('dp')
- global_norm: float32 [], replicated
- momentum_first: float32 [2048], P('dp')
- momentum_query: float32 [2048, 2048], P('dp', 'shard')
- momentum_key: float32 [2048, 512], P('dp', 'shard')
- momentum_value: float32 [2048, 512], P('dp', 'shard')
- momentum_output: float32 [2048, 2048], P('shard', 'dp')
- momentum_second: float32 [2048], P('dp')
- momentum_gate: float32 [2048, 8192], P('dp', 'shard')
- momentum_up: float32 [2048, 8192], P('dp', 'shard')
- momentum_down: float32 [8192, 2048], P('shard', 'dp')
- updated_first: float32 [2048], P('dp')
- updated_query: float32 [2048, 2048], P('dp', 'shard')
- updated_key: float32 [2048, 512], P('dp', 'shard')
- updated_value: float32 [2048, 512], P('dp', 'shard')
- updated_output: float32 [2048, 2048], P('shard', 'dp')
- updated_second: float32 [2048], P('dp')
- updated_gate: float32 [2048, 8192], P('dp', 'shard')
- updated_up: float32 [2048, 8192], P('dp', 'shard')
- updated_down: float32 [8192, 2048], P('shard', 'dp')
Inputs may be any that keep to these rules, and one draw needn't show every extreme that they name: `block_ids`: along each row the block numbers never fall, every number 0 to 7 appears, and a block holds 1 to 256 positions.
All inputs are finite; a program needn't handle non-finite values.
Results may differ from a plain program's by a relative error of at most 0.02.
Values may be sent and summed in bfloat16 or wider, within the bound.
A program may use at most 256 MiB of HBM per device.

v0:
```python
import math
import jax
import jax.numpy as jnp
from jax import lax
from jax.sharding import PartitionSpec as P

H = 32
KV = 8
HD = 64
CLIP = 4096
WARMUP = 2000
EPS = 1e-05
THETA = 10000000.0
NEGATIVE = -1e30


def inverse_rms(values):
    return lax.rsqrt(jnp.mean(values * values, axis=1, keepdims=True) + EPS)


def norm_back(values, inverse, gain, grad_normed):
    scaled = grad_normed * gain[None, :]
    gain_grad = jnp.sum(grad_normed * values * inverse, axis=0)
    grad_values = inverse * scaled - values * inverse**3 * jnp.mean(
        scaled * values, axis=1, keepdims=True
    )
    return (gain_grad, grad_values)


def angle_table(count, length):
    positions = (jnp.arange(count, dtype=jnp.int32) % length).astype(jnp.float32)
    powers = -2.0 * jnp.arange(HD // 2, dtype=jnp.float32) / HD
    angles = positions[:, None] * jnp.power(THETA, powers)[None, :]
    return (jnp.cos(angles)[:, None, :], jnp.sin(angles)[:, None, :])


def rotate(values, cosine, sine):
    half = values.shape[-1] // 2
    first = values[..., :half]
    second = values[..., half:]
    return jnp.concatenate(
        [first * cosine - second * sine, second * cosine + first * sine], axis=-1
    )


def unrotate(grads, cosine, sine):
    half = grads.shape[-1] // 2
    first = grads[..., :half]
    second = grads[..., half:]
    return jnp.concatenate(
        [first * cosine + second * sine, second * cosine - first * sine], axis=-1
    )


def to_items(values, seqs, length):
    shaped = values.reshape((seqs, length) + values.shape[1:])
    moved = jnp.moveaxis(shaped, 2, 1)
    return moved.reshape((seqs * values.shape[1], length) + values.shape[2:])


def from_items(items, seqs):
    groups = items.shape[0] // seqs
    shaped = items.reshape((seqs, groups) + items.shape[1:])
    moved = jnp.moveaxis(shaped, 1, 2)
    return moved.reshape((seqs * items.shape[1], groups) + items.shape[2:])


def item_scores(query, key, blocks, scale):
    scores = jnp.einsum("qgd,jd->gqj", query, key, preferred_element_type=jnp.float32) * scale
    allowed = blocks[None, :] <= blocks[:, None]
    return jnp.where(allowed[None], scores, NEGATIVE)


def attend_forward(scale):

    def run(parts):
        query, key, value, blocks = parts
        scores = item_scores(query, key, blocks, scale)
        peak = jnp.max(scores, axis=2, keepdims=True)
        weights = jnp.exp(scores - peak)
        total = jnp.sum(weights, axis=2, keepdims=True)
        probs = (weights / total).astype(jnp.bfloat16)
        mixed = jnp.einsum("gqj,jd->qgd", probs, value, preferred_element_type=jnp.float32)
        return (mixed.astype(jnp.bfloat16), peak, total)

    return run


def attend_backward(scale):

    def run(parts):
        query, key, value, blocks, peak, total, grad_mixed = parts
        scores = item_scores(query, key, blocks, scale)
        probs = jnp.exp(scores - peak) / total
        probs_low = probs.astype(jnp.bfloat16)
        grad_value = jnp.einsum(
            "gqj,qgd->jd", probs_low, grad_mixed, preferred_element_type=jnp.float32
        )
        grad_probs = jnp.einsum(
            "qgd,jd->gqj", grad_mixed, value, preferred_element_type=jnp.float32
        )
        grad_scores = (
            probs * (grad_probs - jnp.sum(probs * grad_probs, axis=2, keepdims=True))
        ).astype(jnp.bfloat16)
        grad_query = (
            jnp.einsum("gqj,jd->qgd", grad_scores, key, preferred_element_type=jnp.float32) * scale
        )
        grad_key = (
            jnp.einsum("gqj,qgd->jd", grad_scores, query, preferred_element_type=jnp.float32)
            * scale
        )
        return (grad_query, grad_key, grad_value)

    return run


def on_device(
    tokens,
    block_ids,
    cotangent,
    gain_first,
    w_query,
    w_key,
    w_value,
    w_output,
    gain_second,
    w_gate,
    w_up,
    w_down,
    moment_first,
    moment_query,
    moment_key,
    moment_value,
    moment_output,
    moment_second,
    moment_gate,
    moment_up,
    moment_down,
    step,
    rate,
):
    seqs, length = block_ids.shape
    count = tokens.shape[0]
    scale = 1.0 / math.sqrt(HD)
    group = H // KV
    (
        gain_one,
        query_weight,
        key_weight,
        value_weight,
        output_weight,
        gain_two,
        gate_weight,
        up_weight,
        down_weight,
    ) = (
        lax.all_gather(gain_first.astype(jnp.bfloat16), "dp", axis=0, tiled=True),
        lax.all_gather(w_query.astype(jnp.bfloat16), "dp", axis=0, tiled=True),
        lax.all_gather(w_key.astype(jnp.bfloat16), "dp", axis=0, tiled=True),
        lax.all_gather(w_value.astype(jnp.bfloat16), "dp", axis=0, tiled=True),
        lax.all_gather(w_output.astype(jnp.bfloat16), "dp", axis=1, tiled=True),
        lax.all_gather(gain_second.astype(jnp.bfloat16), "dp", axis=0, tiled=True),
        lax.all_gather(w_gate.astype(jnp.bfloat16), "dp", axis=0, tiled=True),
        lax.all_gather(w_up.astype(jnp.bfloat16), "dp", axis=0, tiled=True),
        lax.all_gather(w_down.astype(jnp.bfloat16), "dp", axis=1, tiled=True),
    )
    heads_local = query_weight.shape[1] // HD
    kv_local = key_weight.shape[1] // HD
    inputs = tokens.astype(jnp.float32)
    inverse_first = inverse_rms(inputs)
    gain_one_wide = gain_one.astype(jnp.float32)
    normed = (inputs * inverse_first * gain_one_wide[None, :]).astype(jnp.bfloat16)
    cosine, sine = angle_table(count, length)
    query = rotate(
        jnp.dot(normed, query_weight, preferred_element_type=jnp.float32).reshape(
            count, heads_local, HD
        ),
        cosine,
        sine,
    ).astype(jnp.bfloat16)
    key = rotate(
        jnp.dot(normed, key_weight, preferred_element_type=jnp.float32).reshape(
            count, kv_local, HD
        ),
        cosine,
        sine,
    ).astype(jnp.bfloat16)
    value = (
        jnp.dot(normed, value_weight, preferred_element_type=jnp.float32)
        .astype(jnp.bfloat16)
        .reshape(count, kv_local, HD)
    )
    query_items = to_items(query.reshape(count, kv_local, group, HD), seqs, length)
    key_items = to_items(key, seqs, length)
    value_items = to_items(value, seqs, length)
    block_items = jnp.repeat(block_ids, kv_local, axis=0)
    mixed_items, peak, total = lax.map(
        attend_forward(scale), (query_items, key_items, value_items, block_items)
    )
    mixed = from_items(mixed_items, seqs).reshape(count, heads_local * HD)
    hidden = inputs + lax.psum(
        jnp.dot(mixed, output_weight, preferred_element_type=jnp.float32).astype(jnp.bfloat16),
        "shard",
    ).astype(jnp.float32)
    inverse_second = inverse_rms(hidden)
    gain_two_wide = gain_two.astype(jnp.float32)
    normed_two = (hidden * inverse_second * gain_two_wide[None, :]).astype(jnp.bfloat16)
    gate = jnp.dot(normed_two, gate_weight, preferred_element_type=jnp.float32)
    up = jnp.dot(normed_two, up_weight, preferred_element_type=jnp.float32)
    sigmoid_gate = jax.nn.sigmoid(gate)
    activated = (gate * sigmoid_gate * up).astype(jnp.bfloat16)
    result = hidden + lax.psum(
        jnp.dot(activated, down_weight, preferred_element_type=jnp.float32).astype(jnp.bfloat16),
        "shard",
    ).astype(jnp.float32)
    output = result.astype(jnp.bfloat16)
    grad_result = cotangent.astype(jnp.float32)
    grad_down_weight = jnp.einsum(
        "tf,td->fd", activated, cotangent, preferred_element_type=jnp.float32
    )
    grad_act = jnp.einsum("td,fd->tf", cotangent, down_weight, preferred_element_type=jnp.float32)
    grad_gate_in = (grad_act * up * sigmoid_gate * (1.0 + gate * (1.0 - sigmoid_gate))).astype(
        jnp.bfloat16
    )
    grad_up_in = (grad_act * gate * sigmoid_gate).astype(jnp.bfloat16)
    grad_gate_weight = jnp.einsum(
        "tc,tf->cf", normed_two, grad_gate_in, preferred_element_type=jnp.float32
    )
    grad_up_weight = jnp.einsum(
        "tc,tf->cf", normed_two, grad_up_in, preferred_element_type=jnp.float32
    )
    partial_two = jnp.einsum(
        "tf,cf->tc", grad_gate_in, gate_weight, preferred_element_type=jnp.float32
    ) + jnp.einsum("tf,cf->tc", grad_up_in, up_weight, preferred_element_type=jnp.float32)
    grad_normed_two = lax.psum(partial_two.astype(jnp.bfloat16), "shard").astype(jnp.float32)
    gain_grad_two, grad_through = norm_back(hidden, inverse_second, gain_two_wide, grad_normed_two)
    grad_hidden = grad_result + grad_through
    grad_hidden_low = grad_hidden.astype(jnp.bfloat16)
    grad_output_weight = jnp.einsum(
        "tk,td->kd", mixed, grad_hidden_low, preferred_element_type=jnp.float32
    )
    grad_mixed = jnp.einsum(
        "td,kd->tk", grad_hidden_low, output_weight, preferred_element_type=jnp.float32
    ).astype(jnp.bfloat16)
    grad_mixed_items = to_items(grad_mixed.reshape(count, kv_local, group, HD), seqs, length)
    grad_query_items, grad_key_items, grad_value_items = lax.map(
        attend_backward(scale),
        (query_items, key_items, value_items, block_items, peak, total, grad_mixed_items),
    )
    grad_query_in = (
        unrotate(from_items(grad_query_items, seqs).reshape(count, heads_local, HD), cosine, sine)
        .astype(jnp.bfloat16)
        .reshape(count, heads_local * HD)
    )
    grad_key_in = (
        unrotate(from_items(grad_key_items, seqs), cosine, sine)
        .astype(jnp.bfloat16)
        .reshape(count, kv_local * HD)
    )
    grad_value_in = (
        from_items(grad_value_items, seqs).astype(jnp.bfloat16).reshape(count, kv_local * HD)
    )
    grad_query_weight = jnp.einsum(
        "tc,tk->ck", normed, grad_query_in, preferred_element_type=jnp.float32
    )
    grad_key_weight = jnp.einsum(
        "tc,tk->ck", normed, grad_key_in, preferred_element_type=jnp.float32
    )
    grad_value_weight = jnp.einsum(
        "tc,tk->ck", normed, grad_value_in, preferred_element_type=jnp.float32
    )
    partial_one = jnp.einsum(
        "tk,ck->tc", grad_query_in, query_weight, preferred_element_type=jnp.float32
    )
    partial_one = partial_one + jnp.einsum(
        "tk,ck->tc", grad_key_in, key_weight, preferred_element_type=jnp.float32
    )
    partial_one = partial_one + jnp.einsum(
        "tk,ck->tc", grad_value_in, value_weight, preferred_element_type=jnp.float32
    )
    grad_normed = lax.psum(partial_one.astype(jnp.bfloat16), "shard").astype(jnp.float32)
    gain_grad_one, grad_inner = norm_back(inputs, inverse_first, gain_one_wide, grad_normed)
    input_grad = grad_hidden + grad_inner
    owned = (
        lax.psum_scatter(
            gain_grad_one.astype(jnp.bfloat16), "dp", scatter_dimension=0, tiled=True
        ).astype(jnp.float32),
        lax.psum_scatter(
            grad_query_weight.astype(jnp.bfloat16), "dp", scatter_dimension=0, tiled=True
        ).astype(jnp.float32),
        lax.psum_scatter(
            grad_key_weight.astype(jnp.bfloat16), "dp", scatter_dimension=0, tiled=True
        ).astype(jnp.float32),
        lax.psum_scatter(
            grad_value_weight.astype(jnp.bfloat16), "dp", scatter_dimension=0, tiled=True
        ).astype(jnp.float32),
        lax.psum_scatter(
            grad_output_weight.astype(jnp.bfloat16), "dp", scatter_dimension=1, tiled=True
        ).astype(jnp.float32),
        lax.psum_scatter(
            gain_grad_two.astype(jnp.bfloat16), "dp", scatter_dimension=0, tiled=True
        ).astype(jnp.float32),
        lax.psum_scatter(
            grad_gate_weight.astype(jnp.bfloat16), "dp", scatter_dimension=0, tiled=True
        ).astype(jnp.float32),
        lax.psum_scatter(
            grad_up_weight.astype(jnp.bfloat16), "dp", scatter_dimension=0, tiled=True
        ).astype(jnp.float32),
        lax.psum_scatter(
            grad_down_weight.astype(jnp.bfloat16), "dp", scatter_dimension=1, tiled=True
        ).astype(jnp.float32),
    )
    first_shard = (lax.axis_index("shard") == 0).astype(jnp.float32)
    squares = first_shard * (jnp.sum(owned[0] * owned[0]) + jnp.sum(owned[5] * owned[5]))
    for position in (1, 2, 3, 4, 6, 7, 8):
        squares = squares + jnp.sum(owned[position] * owned[position])
    global_norm = jnp.sqrt(lax.psum(squares, ("dp", "shard")))
    factor = jnp.minimum(1.0, CLIP / global_norm)
    rate_now = rate * jnp.minimum(1.0, (step.astype(jnp.float32) + 1.0) / WARMUP)
    masters = (gain_first, w_query, w_key, w_value, w_output, gain_second, w_gate, w_up, w_down)
    moments = (
        moment_first,
        moment_query,
        moment_key,
        moment_value,
        moment_output,
        moment_second,
        moment_gate,
        moment_up,
        moment_down,
    )
    momenta = [0.5 * moment + 0.5 * (factor * gradient) for moment, gradient in zip(moments, owned)]
    updated = [master - rate_now * momentum for master, momentum in zip(masters, momenta)]
    return (
        output,
        input_grad,
        global_norm,
        momenta[0],
        momenta[1],
        momenta[2],
        momenta[3],
        momenta[4],
        momenta[5],
        momenta[6],
        momenta[7],
        momenta[8],
        updated[0],
        updated[1],
        updated[2],
        updated[3],
        updated[4],
        updated[5],
        updated[6],
        updated[7],
        updated[8],
    )


def solution(mesh):
    in_specs = (
        P("dp", None),
        P("dp", None),
        P("dp", None),
        P("dp"),
        P("dp", "shard"),
        P("dp", "shard"),
        P("dp", "shard"),
        P("shard", "dp"),
        P("dp"),
        P("dp", "shard"),
        P("dp", "shard"),
        P("shard", "dp"),
        P("dp"),
        P("dp", "shard"),
        P("dp", "shard"),
        P("dp", "shard"),
        P("shard", "dp"),
        P("dp"),
        P("dp", "shard"),
        P("dp", "shard"),
        P("shard", "dp"),
        P(),
        P(),
    )
    out_specs = (
        P("dp", None),
        P("dp", None),
        P(),
        P("dp"),
        P("dp", "shard"),
        P("dp", "shard"),
        P("dp", "shard"),
        P("shard", "dp"),
        P("dp"),
        P("dp", "shard"),
        P("dp", "shard"),
        P("shard", "dp"),
        P("dp"),
        P("dp", "shard"),
        P("dp", "shard"),
        P("dp", "shard"),
        P("shard", "dp"),
        P("dp"),
        P("dp", "shard"),
        P("dp", "shard"),
        P("shard", "dp"),
    )
    return jax.shard_map(
        on_device, mesh=mesh, in_specs=in_specs, out_specs=out_specs, check_vma=False
    )
```

profile of v0, /device:TPU:0, one launch (start us, length us, event | category | flops | bytes accessed | tf_op | source)
XLA Modules:
  0.0 1819.1 jit_solution(10321602777745166804)
XLA Ops:
  11.8 22.4 %all-gather = bf16[8,1,256]{2,1,0:T(2,128)(2,1)S(1)} all-gather(bf16[1,1,256]{2,1,0:T(2,128)(2,1)S(1)} %reshape.331), channel_id=1, replica_groups=mesh['dp'=8,'shard'=4] {'dp'}, dimensions={0}, use_global_device_ids=true | all-gather | bytes 4608 | tf_op jit(solution)/shard_map/all_gather | solution.py:157
  38.9 32.9 %all_gather.28 = bf16[2048,128]{1,0:T(8,128)(2,1)S(1)} all-gather(bf16[256,128]{1,0:T(8,128)(2,1)S(1)} %convert_element_type.243), channel_id=1, replica_groups=mesh['dp'=8,'shard'=4] {'dp'}, dimensions={0}, use_global_device_ids=true | all-gather | bytes 589824 | tf_op jit(solution)/shard_map/all_gather | solution.py:160
  72.8 31.7 %all_gather.29 = bf16[2048,128]{1,0:T(8,128)(2,1)S(1)} all-gather(bf16[256,128]{1,0:T(8,128)(2,1)S(1)} %convert_element_type.245), channel_id=1, replica_groups=mesh['dp'=8,'shard'=4] {'dp'}, dimensions={0}, use_global_device_ids=true | all-gather | bytes 589824 | tf_op jit(solution)/shard_map/all_gather | solution.py:159
  116.8 30.4 %while.28 = (s32[]{:T(128)}, bf16[2,1024,4,64]{1,3,2,0:T(8,128)(2,1)}, f32[2,4,1024,1]{2,1,3,0:T(4,128)}, f32[2,4,1024,1]{2,1,3,0:T(4,128)}, bf16[2,1024,64]{1,2...) while((s32[]{:T(128)}, ...), condition=%wide.region_4.5_spmd, body=%wide.region_1.4_spmd.sunk | while | flops 1125376000 | bytes 64387236 | solution.py:197
  160.8 16.6 all-gather.1
  177.3 59.9 %all-reduce.8.cloned.1.call-done = bf16[1024,2048]{1,0:T(8,128)(2,1)} async-done(((bf16[1024,2048]{1,0:T(8,128)(2,1)}), bf16[1024,2048]{1,0:T(8,128)(2,1)}) %all-reduce.8.cloned.1.call-update) | async-done | bytes 4194320 | tf_op jit(solution)/shard_map/psum | solution.py:201
  247.8 117.3 %all-gather.12.cloned.1.call-done = bf16[2048,2048]{1,0:T(8,128)(2,1)} async-done(((bf16[256,2048]{1,0:T(8,128)(2,1)}), bf16[2048,2048]{1,0:T(8,128)(2,1)}) %all-gather.12.cloned.1.call-update) | async-done | bytes 8388624 | tf_op jit(solution)/shard_map/all_gather | solution.py:163
  379.6 111.4 %all-gather.14.cloned.1.call-done = bf16[2048,2048]{1,0:T(8,128)(2,1)} async-done(((bf16[256,2048]{1,0:T(8,128)(2,1)}), bf16[2048,2048]{1,0:T(8,128)(2,1)}) %all-gather.14.cloned.1.call-update) | async-done | bytes 8388624 | tf_op jit(solution)/shard_map/all_gather | solution.py:164
  491.0 14.5 fusion.113
  505.5 111.8 %all-gather.16.cloned.1.call-done = bf16[2048,2048]{1,0:T(8,128)(2,1)} async-done(((bf16[2048,256]{1,0:T(8,128)(2,1)}), bf16[2048,2048]{1,0:T(8,128)(2,1)}) %all-gather.16.cloned.1.call-update) | async-done | bytes 8388624 | tf_op jit(solution)/shard_map/all_gather | solution.py:165
  617.3 22.1 %multiply_convert_fusion = (bf16[1024,2048]{1,0:T(8,128)(2,1)}, bf16[1024,2048]{1,0:T(8,128)(2,1)}, bf16[1024,2048]{1,0:T(8,128)(2,1)}) fusion(f32[1024,2048]{1,0:T(8,128)} %fusion.112, f32[1024,2048]{1,0:T(8,128)} %fusion.113, bf16[1024,2048]{1,0:T(8,128)(2,1)} %param.29, bf16[2048,2048]{1,0:T(8,128)(2,1)} %all-gather.16.cloned.1.call-done), kind=kOutput, calls=%fused_computation.96 | convolution fusion | flops 8623489024 | bytes 41943040 | tf_op jit(solution)/shard_map/td,fd->tf/dot_general | solution.py:221
  639.4 14.7 fusion.114
  666.4 83.8 %all-reduce.10.cloned.1.call-done = bf16[1024,2048]{1,0:T(8,128)(2,1)} async-done(((bf16[1024,2048]{1,0:T(8,128)(2,1)}), bf16[1024,2048]{1,0:T(8,128)(2,1)}) %all-reduce.10.cloned.1.call-update) | async-done | bytes 4194320 | tf_op jit(solution)/shard_map/psum | solution.py:235
  767.5 79.0 %while.29 = (s32[]{:T(128)}, f32[2,1024,4,64]{1,3,2,0:T(8,128)}, f32[2,1024,64]{1,2,0:T(8,128)}, bf16[2,1024,64]{1,2,0:T(8,128)(2,1)}, bf16[2,1024,64]{1,2,0:T(8...) while((s32[]{:T(128)}, f32[2,1024,4,64]{1,3,2,0:T(8,128)}, ...), condition=%wide.region_12.13_spmd, body=%wide.region_10.12_spmd.sunk | while | flops 2727669760 | bytes 159401328 | solution.py:246
  937.6 41.8 %reduce-scatter.12.cloned.1.call-done = bf16[256,128]{1,0:T(8,128)(2,1)} async-done(((bf16[2048,128]{1,0:T(8,128)(2,1)}), bf16[256,128]{1,0:T(8,128)(2,1)}) %reduce-scatter.12.cloned.1.call-update) | async-done | bytes 65552 | tf_op jit(solution)/shard_map/reduce_scatter | solution.py:294
  980.9 153.2 %all-reduce.12.cloned.1.call-done = (bf16[1024,2048]{1,0:T(8,128)(2,1)}, bf16[1024,2048]{1,0:T(8,128)(2,1)}) async-done(((bf16[1024,2048]{1,0:T(8,128)(2,1)}, bf16[1024,2048]{1,0:T(8,128)(2,1)}), (bf16[1024,2048]{1,0:T(8,128)(2,1)}, bf16[1024,2048]{1,0:T(8,128)(2,1)})) %all-reduce.12.cloned.1.call-update) | async-done | bytes 8388624 | tf_op jit(solution)/shard_map/psum | solution.py:212
  1139.8 22.3 %all-reduce.2 = (bf16[2048]{0:T(1024)(128)(2,1)S(1)}, bf16[2048]{0:T(1024)(128)(2,1)S(1)}) all-reduce(bf16[2048]{0:T(1024)(128)(2,1)S(1)} %get-tuple-element.132, bf16[2048]{0:T(1024)(128)(2,1)S(1)} %copy-done.43), channel_id=2, replica_groups=mesh['dp'=8,'shard'=4] {'dp'}, use_global_device_ids=true, to_apply=%region_16.17.clone | all-reduce | flops 4096 | bytes 16384
  1164.1 41.8 %reduce-scatter.8.cloned.1.call-done = bf16[256,512]{1,0:T(8,128)(2,1)} async-done(((bf16[2048,512]{1,0:T(8,128)(2,1)}), bf16[256,512]{1,0:T(8,128)(2,1)}) %reduce-scatter.8.cloned.1.call-update) | async-done | bytes 262160 | tf_op jit(solution)/shard_map/reduce_scatter | solution.py:288
  1209.5 67.7 %reduce-scatter.14.cloned.1.call-done = bf16[512,256]{1,0:T(8,128)(2,1)} async-done(((bf16[512,2048]{1,0:T(8,128)(2,1)}), bf16[512,256]{1,0:T(8,128)(2,1)}) %reduce-scatter.14.cloned.1.call-update) | async-done | bytes 262160 | tf_op jit(solution)/shard_map/reduce_scatter | solution.py:297
  1280.1 148.8 %reduce-scatter.16.cloned.1.call-done = bf16[256,2048]{1,0:T(8,128)(2,1)} async-done(((bf16[2048,2048]{1,0:T(8,128)(2,1)}), bf16[256,2048]{1,0:T(8,128)(2,1)}) %reduce-scatter.16.cloned.1.call-update) | async-done | bytes 1048592 | tf_op jit(solution)/shard_map/reduce_scatter | solution.py:303
  1431.9 148.9 %reduce-scatter.18.cloned.1.call-done = bf16[256,2048]{1,0:T(8,128)(2,1)} async-done(((bf16[2048,2048]{1,0:T(8,128)(2,1)}), bf16[256,2048]{1,0:T(8,128)(2,1)}) %reduce-scatter.18.cloned.1.call-update) | async-done | bytes 1048592 | tf_op jit(solution)/shard_map/reduce_scatter | solution.py:306
  1583.9 148.9 %reduce-scatter.20.cloned.1.call-done = bf16[2048,256]{1,0:T(8,128)(2,1)} async-done(((bf16[2048,2048]{1,0:T(8,128)(2,1)}), bf16[2048,256]{1,0:T(8,128)(2,1)}) %reduce-scatter.20.cloned.1.call-update) | async-done | bytes 1048592 | tf_op jit(solution)/shard_map/reduce_scatter | solution.py:309
  1735.9 14.7 fusion.60
  1750.7 39.0 %psum.39 = f32[]{:T(128)} all-reduce(f32[]{:T(128)S(6)} %add.221), channel_id=1, replica_groups=mesh['dp'=8,'shard'=4] {'dp','shard'}, use_global_device_ids=true, to_apply=%region_35.36 | all-reduce | flops 1 | bytes 8 | tf_op jit(solution)/shard_map/psum | solution.py:317
  (269 shorter events, 327.5 us)
Async XLA Ops:
  7.2 103.3 %all-gather.8.cloned.1.call-start = ((), (), s32[]{:S(2)}) async-start(), calls=%async_computation.7 | async-start | bytes 2359296 | tf_op jit(solution)/shard_map/all_gather | solution.py:158
  9.0 138.2 %all-gather.10.cloned.1.call-start = ((), (), s32[]{:S(2)}) async-start(), calls=%async_computation.8 | async-start | bytes 2359296 | tf_op jit(solution)/shard_map/all_gather | solution.py:161
  10.9 226.4 %all-reduce.8.cloned.1.call-start = ((), (), s32[]{:S(2)}) async-start(), calls=%async_computation.9 | async-start | bytes 8388608 | tf_op jit(solution)/shard_map/psum | solution.py:201
  11.0 93.5 %copy-start = (bf16[1024,2048]{1,0:T(8,128)(2,1)S(1)}, bf16[1024,2048]{1,0:T(8,128)(2,1)}, u32[]{:S(2)}) copy-start(bf16[1024,2048]{1,0:T(8,128)(2,1)} %param.27) | copy-start | bytes 12582916
  154.0 211.2 %all-gather.12.cloned.1.call-start = ((), (), s32[]{:S(2)}) async-start(), calls=%async_computation.10 | async-start | bytes 9437184 | tf_op jit(solution)/shard_map/all_gather | solution.py:163
  155.2 335.8 %all-gather.14.cloned.1.call-start = ((), (), s32[]{:S(2)}) async-start(), calls=%async_computation.11 | async-start | bytes 9437184 | tf_op jit(solution)/shard_map/all_gather | solution.py:164
  157.9 459.3 %all-gather.16.cloned.1.call-start = ((), (), s32[]{:S(2)}) async-start(), calls=%async_computation.12 | async-start | bytes 9437184 | tf_op jit(solution)/shard_map/all_gather | solution.py:165
  160.7 589.4 %all-reduce.10.cloned.1.call-start = ((), (), s32[]{:S(2)}) async-start(), calls=%async_computation.13 | async-start | bytes 8388608 | tf_op jit(solution)/shard_map/psum | solution.py:235
  666.3 269.8 %reduce-scatter.10.cloned.1.call-start = ((), (), s32[]{:S(2)}) async-start(), calls=%async_computation.15 | async-start | bytes 589824 | tf_op jit(solution)/shard_map/reduce_scatter | solution.py:291
  767.5 79.0 %copy-start.23 = (f32[1024,32]{0,1:T(8,128)S(1)}, f32[1024,32]{0,1:T(8,128)}, u32[]{:S(2)}) copy-start(f32[1024,32]{0,1:T(8,128)} %copy-done.22) | copy-start | bytes 393220
  767.5 79.0 %copy-start.25 = (f32[1024,32]{0,1:T(8,128)S(1)}, f32[1024,32]{0,1:T(8,128)}, u32[]{:S(2)}) copy-start(f32[1024,32]{0,1:T(8,128)} %copy-done.24) | copy-start | bytes 393220
  852.0 127.5 %reduce-scatter.12.cloned.1.call-start = ((), (), s32[]{:S(2)}) async-start(), calls=%async_computation.16 | async-start | bytes 589824 | tf_op jit(solution)/shard_map/reduce_scatter | solution.py:294
  868.6 265.5 %all-reduce.12.cloned.1.call-start = ((), (), s32[]{:S(2)}) async-start(), calls=%async_computation.21 | async-start | bytes 16777216 | tf_op jit(solution)/shard_map/psum | solution.py:212
  877.3 328.6 %reduce-scatter.8.cloned.1.call-start = ((), (), s32[]{:S(2)}) async-start(), calls=%async_computation.14 | async-start | bytes 2359296 | tf_op jit(solution)/shard_map/reduce_scatter | solution.py:288
  883.6 393.6 %reduce-scatter.14.cloned.1.call-start = ((), (), s32[]{:S(2)}) async-start(), calls=%async_computation.17 | async-start | bytes 2359296 | tf_op jit(solution)/shard_map/reduce_scatter | solution.py:297
  890.7 538.2 %reduce-scatter.16.cloned.1.call-start = ((), (), s32[]{:S(2)}) async-start(), calls=%async_computation.18 | async-start | bytes 9437184 | tf_op jit(solution)/shard_map/reduce_scatter | solution.py:303
  904.8 676.1 %reduce-scatter.18.cloned.1.call-start = ((), (), s32[]{:S(2)}) async-start(), calls=%async_computation.19 | async-start | bytes 9437184 | tf_op jit(solution)/shard_map/reduce_scatter | solution.py:306
  919.4 813.5 %reduce-scatter.20.cloned.1.call-start = ((), (), s32[]{:S(2)}) async-start(), calls=%async_computation.20 | async-start | bytes 9437184 | tf_op jit(solution)/shard_map/reduce_scatter | solution.py:309
  933.5 200.6 %copy-start.39 = (f32[8,1,256]{2,1,0:T(1,128)S(1)}, f32[8,1,256]{2,1,0:T(1,128)}, u32[]{:S(2)}) copy-start(f32[8,1,256]{2,1,0:T(1,128)} %copy-done.38) | copy-start | bytes 24580
  933.5 200.6 %copy-start.41 = (f32[1024]{0:T(1024)S(1)}, f32[1024]{0:T(1024)}, u32[]{:S(2)}) copy-start(f32[1024]{0:T(1024)} %copy-done.40) | copy-start | bytes 12292
  933.5 206.3 %copy-start.43 = (bf16[2048]{0:T(1024)(128)(2,1)S(1)}, bf16[2048]{0:T(1024)(128)(2,1)}, u32[]{:S(2)}) copy-start(bf16[2048]{0:T(1024)(128)(2,1)} %get-tuple-element.130) | copy-start | bytes 12292
  933.5 802.4 %copy-start.42 = (f32[1024]{0:T(1024)S(1)}, f32[1024]{0:T(1024)}, u32[]{:S(2)}) copy-start(f32[1024]{0:T(1024)} %get-tuple-element.217) | copy-start | bytes 12292
  1162.1 573.8 %copy-start.46 = (bf16[2048]{0:T(1024)(128)(2,1)}, bf16[2048]{0:T(1024)(128)(2,1)S(1)}, u32[]{:S(2)}) copy-start(bf16[2048]{0:T(1024)(128)(2,1)S(1)} %get-tuple-element.173) | copy-start | bytes 12292
  1162.1 573.8 %copy-start.47 = (bf16[2048]{0:T(1024)(128)(2,1)}, bf16[2048]{0:T(1024)(128)(2,1)S(1)}, u32[]{:S(2)}) copy-start(bf16[2048]{0:T(1024)(128)(2,1)S(1)} %get-tuple-element.172) | copy-start | bytes 12292
  (55 other events, 741.9 us)
Sparse Core Ops, SparseCore 0:
  10.7 58.7 all-gather.7
  72.2 52.4 all-gather.9
  154.1 83.1 all-reduce.7
  240.0 125.0 all-gather.11
  367.9 123.0 all-gather.13
  493.7 123.5 all-gather.15
  666.4 83.6 all-reduce.9
  852.1 62.0 reduce-scatter.9
  918.5 60.9 reduce-scatter.11
  981.9 152.2 all-reduce.11
  1138.2 67.5 reduce-scatter.7
  1209.8 67.3 reduce-scatter.13
  1280.8 148.0 reduce-scatter.15
  1432.8 148.0 reduce-scatter.17
  1584.4 148.4 reduce-scatter.19
where the time goes:
time: 1830 us; the launch traced here: 1820 us
  waiting for transfers between devices  1240 us (68%)
  matrix products  253 us (14%)
  blocking collectives  165 us (9%)
  other arithmetic  126 us (7%)
  between operations  24.5 us (1%)
    psum x1, waiting for transfers between devices, on_device(): lax.psum(jnp.dot(activated, down_weight, preferred_element_type=jnp.float...  153 us
    reduce_scatter x1, waiting for transfers between devices, on_device(): lax.psum_scatter(grad_up_weight.astype(jnp.bfloat16), 'dp', scatter_dimen...  149 us
    reduce_scatter x1, waiting for transfers between devices, on_device(): lax.psum_scatter(grad_down_weight.astype(jnp.bfloat16), 'dp', scatter_dim...  149 us
    reduce_scatter x1, waiting for transfers between devices, on_device(): lax.psum_scatter(grad_gate_weight.astype(jnp.bfloat16), 'dp', scatter_dim...  149 us
    all_gather x1, waiting for transfers between devices, on_device(): lax.all_gather(w_gate.astype(jnp.bfloat16), 'dp', axis=0, tiled=True)  117 us
    all_gather x1, waiting for transfers between devices, on_device(): lax.all_gather(w_down.astype(jnp.bfloat16), 'dp', axis=1, tiled=True)  112 us
    all_gather x1, waiting for transfers between devices, on_device(): lax.all_gather(w_up.astype(jnp.bfloat16), 'dp', axis=0, tiled=True)  111 us
    psum x1, waiting for transfers between devices, on_device(): lax.psum(partial_two.astype(jnp.bfloat16), 'shard').astype(jnp.float32)  83.8 us
  transfers between devices with their start and end apart: 15, of which 12 were waited for; matrix products, arithmetic and copies ran while one was open for 11% of the time, Pallas kernels for 0%

commit v1 on v0

--- a/solution.py
+++ b/solution.py
@@ -12,6 +12,10 @@
 EPS = 1e-05
 THETA = 10000000.0
 NEGATIVE = -1e30
+
+
+def change_leaves(vals):
+    return lax.psum(lax.psum(vals, "shard"), "dp")
 
 
 def inverse_rms(values):
@@ -314,7 +318,7 @@
     squares = first_shard * (jnp.sum(owned[0] * owned[0]) + jnp.sum(owned[5] * owned[5]))
     for position in (1, 2, 3, 4, 6, 7, 8):
         squares = squares + jnp.sum(owned[position] * owned[position])
-    global_norm = jnp.sqrt(lax.psum(squares, ("dp", "shard")))
+    global_norm = jnp.sqrt(change_leaves(squares))
     factor = jnp.minimum(1.0, CLIP / global_norm)
     rate_now = rate * jnp.minimum(1.0, (step.astype(jnp.float32) + 1.0) / WARMUP)
     masters = (gain_first, w_query, w_key, w_value, w_output, gain_second, w_gate, w_up, w_down)

time: 1830 us -> 1820 us (level)
    psum x1 -> x2, blocking collectives: 39 us -> 27.4 us  [change_leaves(): return lax.psum(lax.psum(vals, 'shard'), 'dp')]
where the time goes in v1:
time: 1820 us; the launch traced here: 1810 us
  waiting for transfers between devices  1240 us (68%)
  matrix products  253 us (14%)
  blocking collectives  153 us (8%)
  other arithmetic  126 us (7%)
  between operations  24.5 us (1%)
    psum x1, waiting for transfers between devices, on_device(): lax.psum(jnp.dot(activated, down_weight, preferred_element_type=jnp.float...  153 us
    reduce_scatter x1, waiting for transfers between devices, on_device(): lax.psum_scatter(grad_gate_weight.astype(jnp.bfloat16), 'dp', scatter_dim...  149 us
    reduce_scatter x1, waiting for transfers between devices, on_device(): lax.psum_scatter(grad_up_weight.astype(jnp.bfloat16), 'dp', scatter_dimen...  149 us
    reduce_scatter x1, waiting for transfers between devices, on_device(): lax.psum_scatter(grad_down_weight.astype(jnp.bfloat16), 'dp', scatter_dim...  149 us
    all_gather x1, waiting for transfers between devices, on_device(): lax.all_gather(w_gate.astype(jnp.bfloat16), 'dp', axis=0, tiled=True)  117 us
    all_gather x1, waiting for transfers between devices, on_device(): lax.all_gather(w_down.astype(jnp.bfloat16), 'dp', axis=1, tiled=True)  112 us
    all_gather x1, waiting for transfers between devices, on_device(): lax.all_gather(w_up.astype(jnp.bfloat16), 'dp', axis=0, tiled=True)  111 us
    psum x1, waiting for transfers between devices, on_device(): lax.psum(partial_two.astype(jnp.bfloat16), 'shard').astype(jnp.float32)  83.8 us
  transfers between devices with their start and end apart: 15, of which 12 were waited for; matrix products, arithmetic and copies ran while one was open for 11% of the time, Pallas kernels for 0%

profile of v1, /device:TPU:0, one launch (start us, length us, event | category | flops | bytes accessed | tf_op | source)
XLA Modules:
  0.0 1807.8 jit_solution(323876094008166666)
XLA Ops:
  11.8 22.4 %all-gather = bf16[8,1,256]{2,1,0:T(2,128)(2,1)S(1)} all-gather(bf16[1,1,256]{2,1,0:T(2,128)(2,1)S(1)} %reshape.331), channel_id=1, replica_groups=mesh['dp'=8,'shard'=4] {'dp'}, dimensions={0}, use_global_device_ids=true | all-gather | bytes 4608 | tf_op jit(solution)/shard_map/all_gather | solution.py:161
  38.9 32.9 %all_gather.28 = bf16[2048,128]{1,0:T(8,128)(2,1)S(1)} all-gather(bf16[256,128]{1,0:T(8,128)(2,1)S(1)} %convert_element_type.243), channel_id=1, replica_groups=mesh['dp'=8,'shard'=4] {'dp'}, dimensions={0}, use_global_device_ids=true | all-gather | bytes 589824 | tf_op jit(solution)/shard_map/all_gather | solution.py:164
  72.8 31.9 %all_gather.29 = bf16[2048,128]{1,0:T(8,128)(2,1)S(1)} all-gather(bf16[256,128]{1,0:T(8,128)(2,1)S(1)} %convert_element_type.245), channel_id=1, replica_groups=mesh['dp'=8,'shard'=4] {'dp'}, dimensions={0}, use_global_device_ids=true | all-gather | bytes 589824 | tf_op jit(solution)/shard_map/all_gather | solution.py:163
  116.9 30.4 %while.28 = (s32[]{:T(128)}, bf16[2,1024,4,64]{1,3,2,0:T(8,128)(2,1)}, f32[2,4,1024,1]{2,1,3,0:T(4,128)}, f32[2,4,1024,1]{2,1,3,0:T(4,128)}, bf16[2,1024,64]{1,2...) while((s32[]{:T(128)}, ...), condition=%wide.region_4.5_spmd, body=%wide.region_1.4_spmd.sunk | while | flops 1125376000 | bytes 64387236 | solution.py:201
  161.0 16.3 all-gather.1
  177.3 59.8 %all-reduce.8.cloned.1.call-done = bf16[1024,2048]{1,0:T(8,128)(2,1)} async-done(((bf16[1024,2048]{1,0:T(8,128)(2,1)}), bf16[1024,2048]{1,0:T(8,128)(2,1)}) %all-reduce.8.cloned.1.call-update) | async-done | bytes 4194320 | tf_op jit(solution)/shard_map/psum | solution.py:205
  247.6 117.3 %all-gather.12.cloned.1.call-done = bf16[2048,2048]{1,0:T(8,128)(2,1)} async-done(((bf16[256,2048]{1,0:T(8,128)(2,1)}), bf16[2048,2048]{1,0:T(8,128)(2,1)}) %all-gather.12.cloned.1.call-update) | async-done | bytes 8388624 | tf_op jit(solution)/shard_map/all_gather | solution.py:167
  364.9 14.5 fusion.112
  379.4 111.4 %all-gather.14.cloned.1.call-done = bf16[2048,2048]{1,0:T(8,128)(2,1)} async-done(((bf16[256,2048]{1,0:T(8,128)(2,1)}), bf16[2048,2048]{1,0:T(8,128)(2,1)}) %all-gather.14.cloned.1.call-update) | async-done | bytes 8388624 | tf_op jit(solution)/shard_map/all_gather | solution.py:168
  505.2 111.9 %all-gather.16.cloned.1.call-done = bf16[2048,2048]{1,0:T(8,128)(2,1)} async-done(((bf16[2048,256]{1,0:T(8,128)(2,1)}), bf16[2048,2048]{1,0:T(8,128)(2,1)}) %all-gather.16.cloned.1.call-update) | async-done | bytes 8388624 | tf_op jit(solution)/shard_map/all_gather | solution.py:169
  617.1 22.1 %multiply_convert_fusion = (bf16[1024,2048]{1,0:T(8,128)(2,1)}, bf16[1024,2048]{1,0:T(8,128)(2,1)}, bf16[1024,2048]{1,0:T(8,128)(2,1)}) fusion(f32[1024,2048]{1,0:T(8,128)} %fusion.112, f32[1024,2048]{1,0:T(8,128)} %fusion.113, bf16[1024,2048]{1,0:T(8,128)(2,1)} %param.29, bf16[2048,2048]{1,0:T(8,128)(2,1)} %all-gather.16.cloned.1.call-done), kind=kOutput, calls=%fused_computation.96 | convolution fusion | flops 8623489024 | bytes 41943040 | tf_op jit(solution)/shard_map/td,fd->tf/dot_general | solution.py:225
  639.1 14.7 fusion.114
  666.2 83.8 %all-reduce.10.cloned.1.call-done = bf16[1024,2048]{1,0:T(8,128)(2,1)} async-done(((bf16[1024,2048]{1,0:T(8,128)(2,1)}), bf16[1024,2048]{1,0:T(8,128)(2,1)}) %all-reduce.10.cloned.1.call-update) | async-done | bytes 4194320 | tf_op jit(solution)/shard_map/psum | solution.py:239
  767.4 78.9 %while.29 = (s32[]{:T(128)}, f32[2,1024,4,64]{1,3,2,0:T(8,128)}, f32[2,1024,64]{1,2,0:T(8,128)}, bf16[2,1024,64]{1,2,0:T(8,128)(2,1)}, bf16[2,1024,64]{1,2,0:T(8...) while((s32[]{:T(128)}, f32[2,1024,4,64]{1,3,2,0:T(8,128)}, ...), condition=%wide.region_12.13_spmd, body=%wide.region_10.12_spmd.sunk | while | flops 2727669760 | bytes 159401328 | solution.py:250
  937.5 41.7 %reduce-scatter.12.cloned.1.call-done = bf16[256,128]{1,0:T(8,128)(2,1)} async-done(((bf16[2048,128]{1,0:T(8,128)(2,1)}), bf16[256,128]{1,0:T(8,128)(2,1)}) %reduce-scatter.12.cloned.1.call-update) | async-done | bytes 65552 | tf_op jit(solution)/shard_map/reduce_scatter | solution.py:298
  980.7 153.2 %all-reduce.12.cloned.1.call-done = (bf16[1024,2048]{1,0:T(8,128)(2,1)}, bf16[1024,2048]{1,0:T(8,128)(2,1)}) async-done(((bf16[1024,2048]{1,0:T(8,128)(2,1)}, bf16[1024,2048]{1,0:T(8,128)(2,1)}), (bf16[1024,2048]{1,0:T(8,128)(2,1)}, bf16[1024,2048]{1,0:T(8,128)(2,1)})) %all-reduce.12.cloned.1.call-update) | async-done | bytes 8388624 | tf_op jit(solution)/shard_map/psum | solution.py:216
  1139.6 22.3 %all-reduce.2 = (bf16[2048]{0:T(1024)(128)(2,1)S(1)}, bf16[2048]{0:T(1024)(128)(2,1)S(1)}) all-reduce(bf16[2048]{0:T(1024)(128)(2,1)S(1)} %get-tuple-element.132, bf16[2048]{0:T(1024)(128)(2,1)S(1)} %copy-done.43), channel_id=2, replica_groups=mesh['dp'=8,'shard'=4] {'dp'}, use_global_device_ids=true, to_apply=%region_16.17.clone | all-reduce | flops 4096 | bytes 16384
  1163.9 41.8 %reduce-scatter.8.cloned.1.call-done = bf16[256,512]{1,0:T(8,128)(2,1)} async-done(((bf16[2048,512]{1,0:T(8,128)(2,1)}), bf16[256,512]{1,0:T(8,128)(2,1)}) %reduce-scatter.8.cloned.1.call-update) | async-done | bytes 262160 | tf_op jit(solution)/shard_map/reduce_scatter | solution.py:292
  1209.3 67.7 %reduce-scatter.14.cloned.1.call-done = bf16[512,256]{1,0:T(8,128)(2,1)} async-done(((bf16[512,2048]{1,0:T(8,128)(2,1)}), bf16[512,256]{1,0:T(8,128)(2,1)}) %reduce-scatter.14.cloned.1.call-update) | async-done | bytes 262160 | tf_op jit(solution)/shard_map/reduce_scatter | solution.py:301
  1279.3 149.4 %reduce-scatter.16.cloned.1.call-done = bf16[256,2048]{1,0:T(8,128)(2,1)} async-done(((bf16[2048,2048]{1,0:T(8,128)(2,1)}), bf16[256,2048]{1,0:T(8,128)(2,1)}) %reduce-scatter.16.cloned.1.call-update) | async-done | bytes 1048592 | tf_op jit(solution)/shard_map/reduce_scatter | solution.py:307
  1431.8 148.9 %reduce-scatter.18.cloned.1.call-done = bf16[256,2048]{1,0:T(8,128)(2,1)} async-done(((bf16[2048,2048]{1,0:T(8,128)(2,1)}), bf16[256,2048]{1,0:T(8,128)(2,1)}) %reduce-scatter.18.cloned.1.call-update) | async-done | bytes 1048592 | tf_op jit(solution)/shard_map/reduce_scatter | solution.py:310
  1583.7 148.9 %reduce-scatter.20.cloned.1.call-done = bf16[2048,256]{1,0:T(8,128)(2,1)} async-done(((bf16[2048,2048]{1,0:T(8,128)(2,1)}), bf16[2048,256]{1,0:T(8,128)(2,1)}) %reduce-scatter.20.cloned.1.call-update) | async-done | bytes 1048592 | tf_op jit(solution)/shard_map/reduce_scatter | solution.py:313
  1743.7 14.7 fusion.60
  1758.4 20.1 %psum.47 = f32[]{:T(128)} all-reduce(f32[]{:T(128)} %psum.46), channel_id=1, replica_groups=mesh['dp'=8,'shard'=4] {'dp'}, use_global_device_ids=true, to_apply=%region_36.37 | all-reduce | flops 1 | bytes 8 | tf_op jit(solution)/shard_map/psum | solution.py:18
  (270 shorter events, 334.9 us)
Async XLA Ops:
  7.2 103.4 %all-gather.8.cloned.1.call-start = ((), (), s32[]{:S(2)}) async-start(), calls=%async_computation.7 | async-start | bytes 2359296 | tf_op jit(solution)/shard_map/all_gather | solution.py:162
  9.0 138.3 %all-gather.10.cloned.1.call-start = ((), (), s32[]{:S(2)}) async-start(), calls=%async_computation.8 | async-start | bytes 2359296 | tf_op jit(solution)/shard_map/all_gather | solution.py:165
  10.9 226.2 %all-reduce.8.cloned.1.call-start = ((), (), s32[]{:S(2)}) async-start(), calls=%async_computation.9 | async-start | bytes 8388608 | tf_op jit(solution)/shard_map/psum | solution.py:205
  11.0 93.7 %copy-start = (bf16[1024,2048]{1,0:T(8,128)(2,1)S(1)}, bf16[1024,2048]{1,0:T(8,128)(2,1)}, u32[]{:S(2)}) copy-start(bf16[1024,2048]{1,0:T(8,128)(2,1)} %param.27) | copy-start | bytes 12582916
  154.1 210.8 %all-gather.12.cloned.1.call-start = ((), (), s32[]{:S(2)}) async-start(), calls=%async_computation.10 | async-start | bytes 9437184 | tf_op jit(solution)/shard_map/all_gather | solution.py:167
  155.3 335.5 %all-gather.14.cloned.1.call-start = ((), (), s32[]{:S(2)}) async-start(), calls=%async_computation.11 | async-start | bytes 9437184 | tf_op jit(solution)/shard_map/all_gather | solution.py:168
  158.2 458.9 %all-gather.16.cloned.1.call-start = ((), (), s32[]{:S(2)}) async-start(), calls=%async_computation.12 | async-start | bytes 9437184 | tf_op jit(solution)/shard_map/all_gather | solution.py:169
  160.9 589.0 %all-reduce.10.cloned.1.call-start = ((), (), s32[]{:S(2)}) async-start(), calls=%async_computation.13 | async-start | bytes 8388608 | tf_op jit(solution)/shard_map/psum | solution.py:239
  666.1 269.9 %reduce-scatter.10.cloned.1.call-start = ((), (), s32[]{:S(2)}) async-start(), calls=%async_computation.15 | async-start | bytes 589824 | tf_op jit(solution)/shard_map/reduce_scatter | solution.py:295
  767.4 78.9 %copy-start.23 = (f32[1024,32]{0,1:T(8,128)S(1)}, f32[1024,32]{0,1:T(8,128)}, u32[]{:S(2)}) copy-start(f32[1024,32]{0,1:T(8,128)} %copy-done.22) | copy-start | bytes 393220
  767.4 78.9 %copy-start.25 = (f32[1024,32]{0,1:T(8,128)S(1)}, f32[1024,32]{0,1:T(8,128)}, u32[]{:S(2)}) copy-start(f32[1024,32]{0,1:T(8,128)} %copy-done.24) | copy-start | bytes 393220
  851.8 127.5 %reduce-scatter.12.cloned.1.call-start = ((), (), s32[]{:S(2)}) async-start(), calls=%async_computation.16 | async-start | bytes 589824 | tf_op jit(solution)/shard_map/reduce_scatter | solution.py:298
  868.5 265.5 %all-reduce.12.cloned.1.call-start = ((), (), s32[]{:S(2)}) async-start(), calls=%async_computation.21 | async-start | bytes 16777216 | tf_op jit(solution)/shard_map/psum | solution.py:216
  877.1 328.5 %reduce-scatter.8.cloned.1.call-start = ((), (), s32[]{:S(2)}) async-start(), calls=%async_computation.14 | async-start | bytes 2359296 | tf_op jit(solution)/shard_map/reduce_scatter | solution.py:292
  883.4 393.6 %reduce-scatter.14.cloned.1.call-start = ((), (), s32[]{:S(2)}) async-start(), calls=%async_computation.17 | async-start | bytes 2359296 | tf_op jit(solution)/shard_map/reduce_scatter | solution.py:301
  890.5 538.2 %reduce-scatter.16.cloned.1.call-start = ((), (), s32[]{:S(2)}) async-start(), calls=%async_computation.18 | async-start | bytes 9437184 | tf_op jit(solution)/shard_map/reduce_scatter | solution.py:307
  904.7 676.0 %reduce-scatter.18.cloned.1.call-start = ((), (), s32[]{:S(2)}) async-start(), calls=%async_computation.19 | async-start | bytes 9437184 | tf_op jit(solution)/shard_map/reduce_scatter | solution.py:310
  919.3 813.4 %reduce-scatter.20.cloned.1.call-start = ((), (), s32[]{:S(2)}) async-start(), calls=%async_computation.20 | async-start | bytes 9437184 | tf_op jit(solution)/shard_map/reduce_scatter | solution.py:313
  933.4 200.6 %copy-start.39 = (f32[8,1,256]{2,1,0:T(1,128)S(1)}, f32[8,1,256]{2,1,0:T(1,128)}, u32[]{:S(2)}) copy-start(f32[8,1,256]{2,1,0:T(1,128)} %copy-done.38) | copy-start | bytes 24580
  933.4 200.6 %copy-start.41 = (f32[1024]{0:T(1024)S(1)}, f32[1024]{0:T(1024)}, u32[]{:S(2)}) copy-start(f32[1024]{0:T(1024)} %copy-done.40) | copy-start | bytes 12292
  933.4 206.2 %copy-start.43 = (bf16[2048]{0:T(1024)(128)(2,1)S(1)}, bf16[2048]{0:T(1024)(128)(2,1)}, u32[]{:S(2)}) copy-start(bf16[2048]{0:T(1024)(128)(2,1)} %get-tuple-element.130) | copy-start | bytes 12292
  933.4 810.2 %copy-start.42 = (f32[1024]{0:T(1024)S(1)}, f32[1024]{0:T(1024)}, u32[]{:S(2)}) copy-start(f32[1024]{0:T(1024)} %get-tuple-element.217) | copy-start | bytes 12292
  1161.9 581.8 %copy-start.46 = (bf16[2048]{0:T(1024)(128)(2,1)}, bf16[2048]{0:T(1024)(128)(2,1)S(1)}, u32[]{:S(2)}) copy-start(bf16[2048]{0:T(1024)(128)(2,1)S(1)} %get-tuple-element.173) | copy-start | bytes 12292
  1161.9 581.7 %copy-start.47 = (bf16[2048]{0:T(1024)(128)(2,1)}, bf16[2048]{0:T(1024)(128)(2,1)S(1)}, u32[]{:S(2)}) copy-start(bf16[2048]{0:T(1024)(128)(2,1)S(1)} %get-tuple-element.172) | copy-start | bytes 12292
  (55 other events, 666.7 us)
Sparse Core Ops, SparseCore 0:
  10.7 58.5 all-gather.7
  71.9 52.7 all-gather.9
  154.2 82.7 all-reduce.7
  239.8 125.0 all-gather.11
  367.7 123.0 all-gather.13
  493.4 123.5 all-gather.15
  666.2 83.6 all-reduce.9
  851.9 61.9 reduce-scatter.9
  918.2 61.0 reduce-scatter.11
  981.7 152.2 all-reduce.11
  1138.0 67.5 reduce-scatter.7
  1209.6 67.3 reduce-scatter.13
  1280.6 148.0 reduce-scatter.15
  1432.7 148.0 reduce-scatter.17
  1584.2 148.4 reduce-scatter.19
